TPU v7x, 32 devices: a whole 2x2x4 slice. The times are simulated.
32 devices in a mesh: section: 2 (over x), dp: 16 (over z, y, core).
Axes of the slice: x: 2, y: 2, z: 4, core: 2. Of those that a mesh axis runs over, the one named last changes fastest.
Arguments:
- section_rows: bfloat16 [2, 2048, 1024], P('section', 'dp'), may hold values from -6 to 6
- lang_ids: int32 [2048], P('dp'), may hold values from 0 to 199, as said below
- lang_table: int32 [200], replicated, may hold values from 0 to 7, as said below
- lang_counts: int32 [16, 200], P('dp'), may hold values from 4 to 210
- temp_num: int32 [200], replicated, may hold values from 1 to 16
- weights: bfloat16 [2, 1024, 32768], P('section', None, 'dp'), may hold values from -0.1875 to 0.1875
Outputs:
- grads: float32 [2, 1024, 32768], P('section', None, 'dp')
- input_grad: bfloat16 [2048, 1024], P('dp', 'section')
Inputs may be any that keep to these rules, and one draw needn't show every extreme that they name: `lang_table`: every block is named by at least one language. `lang_ids`: on each replica (each aligned block of 128 rows) at most 32 rows map to any one block through lang_table, and one block receives exactly 32 rows from every replica.
All inputs are finite; a program needn't handle non-finite values.
Results may differ from a plain program's by a relative error of at most 0.0058.
Values may be sent and summed in bfloat16 or wider, within the bound.
No kernel may reach another device: no remote copies, remote signals or barrier semaphores. Data moves between devices by JAX's collectives and lax.ppermute only.
A program may use at most 64 MiB of HBM per device.

v0:
```python
import jax
import jax.numpy as jnp
from jax import lax
from jax.sharding import PartitionSpec as P


def partner(value, axis, bit):
    mask = 2**bit
    pairs = [(source, source ^ mask) for source in range(lax.axis_size(axis))]
    return lax.ppermute(value, axis, pairs)


def shifted(value, axis, steps):
    count = lax.axis_size(axis)
    first, last = (max(0, -steps), min(count, count - steps))
    return lax.ppermute(value, axis, [(source, source + steps) for source in range(first, last)])


def on_device(section_rows, lang_ids, lang_table, lang_counts, temp_num, weights):
    section_pos = lax.axis_index("section")
    replicas = lax.axis_size("dp")
    blocks_all = replicas // 2
    rows_dev = lang_ids.shape[0]
    capacity = 2 * rows_dev // blocks_all
    row_width = section_rows.shape[2]
    half_width = row_width // 2
    languages = lang_table.shape[0]
    own_weight = weights[0]
    lang_hot = lang_ids[:, None] == jnp.arange(languages, dtype=jnp.int32)[None, :]
    row_block = jnp.sum(jnp.where(lang_hot, lang_table[None, :], 0), axis=1)
    block_hot = (row_block[:, None] == jnp.arange(blocks_all, dtype=jnp.int32)[None, :]).astype(
        jnp.int32
    )
    running = jnp.cumsum(block_hot, axis=0) - 1
    slot_index = jnp.sum(running * block_hot, axis=1)
    target = row_block * capacity + slot_index
    placing = target[None, :] == jnp.arange(blocks_all * capacity, dtype=jnp.int32)[:, None]
    totals = lax.psum(lang_counts[0].astype(jnp.float32), "dp")
    lang_scale = 2.0 * replicas * temp_num.astype(jnp.float32) / totals
    row_scale = jnp.sum(jnp.where(lang_hot, lang_scale[None, :], 0.0), axis=1)
    local_rows = section_rows[0]
    weighted = (local_rows * row_scale[:, None]).astype(jnp.bfloat16)
    outgoing = jnp.where(section_pos == 1, weighted, local_rows)
    packed = jnp.dot(
        placing.astype(jnp.bfloat16), outgoing, preferred_element_type=jnp.float32
    ).astype(jnp.bfloat16)
    packed = packed.reshape(blocks_all, capacity, row_width)
    doubled = jnp.repeat(packed, 2, axis=0)
    arrived = lax.all_to_all(doubled, "dp", split_axis=0, concat_axis=0, tiled=True)
    projected = jnp.einsum("skd,df->skf", arrived, own_weight, preferred_element_type=jnp.float32)
    routed_flat = arrived.reshape(-1, row_width)
    projected = projected.reshape(routed_flat.shape[0], -1)
    handed = jnp.where(section_pos == 0, jnp.maximum(projected, 0.0), projected).astype(
        jnp.bfloat16
    )
    received = partner(handed, "section", 0)
    partner_term = jnp.where(
        (section_pos == 0) & (projected <= 0.0), jnp.zeros_like(received), received
    )
    weight_grad = lax.dot_general(
        routed_flat, partner_term, (((0,), (0,)), ((), ())), preferred_element_type=jnp.float32
    )

    def input_terms():
        return lax.dot_general(
            partner_term, own_weight, (((1,), (1,)), ((), ())), preferred_element_type=jnp.float32
        )

    def no_terms():
        return jnp.zeros((routed_flat.shape[0], row_width), jnp.float32)

    partial_rows = lax.cond(section_pos == 0, input_terms, no_terms)
    unplace = placing.astype(jnp.float32)
    came_back = lax.all_to_all(
        partial_rows.reshape(replicas, capacity, row_width),
        "dp",
        split_axis=0,
        concat_axis=0,
        tiled=True,
    )
    summed = (
        came_back.reshape(blocks_all, 2, capacity, row_width)
        .sum(axis=1)
        .reshape(blocks_all * capacity, row_width)
    )
    full_rows = lax.dot_general(
        unplace,
        summed,
        (((0,), (0,)), ((), ())),
        precision=lax.Precision.HIGHEST,
        preferred_element_type=jnp.float32,
    ).astype(jnp.bfloat16)
    right_cols = shifted(full_rows[:, half_width:], "section", 1)
    input_grad = jnp.where(section_pos == 0, full_rows[:, :half_width], right_cols)
    return (weight_grad[None], input_grad)


def solution(mesh):
    return jax.shard_map(
        on_device,
        mesh=mesh,
        in_specs=(
            P("section", "dp", None),
            P("dp"),
            P(),
            P("dp", None),
            P(),
            P("section", None, "dp"),
        ),
        out_specs=(P("section", None, "dp"), P("dp", "section")),
        check_vma=False,
    )
```

profile of v0, /device:TPU:1, one launch (start us, length us, event | category | flops | bytes accessed | tf_op | source)
XLA Modules:
  0.0 195.7 jit_solution(13366520089438789141)
XLA Ops:
  0.6 0.7 convert_element_type.35
  1.3 30.6 %psum.7 = f32[200]{0:T(256)S(1)} all-reduce(f32[200]{0:T(256)S(1)} %bitcast.31), channel_id=1, replica_groups=mesh['section'=2,'dp'=16] {'dp'}, use_global_device_ids=true, to_apply=%region_3.4 | all-reduce | flops 200 | bytes 1600 | tf_op jit(solution)/shard_map/psum | solution.py:38
  31.9 0.8 select_reduce_fusion.1
  32.7 0.7 multiply_divide_fusion
  33.3 0.8 select_reduce_fusion
  34.1 0.1 fusion.8
  34.2 0.2 reduce_window_sum.11
  34.4 0.2 select_reduce_fusion.2
  34.6 1.3 convolution_convert_fusion
  35.9 1.1 broadcast_in_dim.46
  37.0 7.8 %all-to-all-start = ((bf16[16,32,1024]{2,1,0:T(8,128)(2,1)}), bf16[16,32,1024]{2,1,0:T(8,128)(2,1)S(1)}, u32[]{:S(2)}, u32[]{:S(2)}) async-start(bf16[16,32,1024]{2,1,0:T(8,128)(2,1)} %bitcast.3), calls=%async_computation | async-start | bytes 2097152 | tf_op jit(solution)/shard_map/all_to_all | solution.py:49
  44.9 23.2 %all-to-all-done = bf16[16,32,1024]{2,1,0:T(8,128)(2,1)S(1)} async-done(((bf16[16,32,1024]{2,1,0:T(8,128)(2,1)}), bf16[16,32,1024]{2,1,0:T(8,128)(2,1)S(1)}, u32[]{:S(2)}, u32[]{:S(2)}) %all-to-all-start) | async-done | bytes 1048608 | tf_op jit(solution)/shard_map/all_to_all | solution.py:49
  68.0 7.3 %fusion = (bf16[512,2048]{1,0:T(8,128)(2,1)}, f32[512,2048]{1,0:T(8,128)}) fusion(pred[]{:T(512)S(6)} %eq.58, bf16[512,1024]{1,0:T(8,128)(2,1)S(1)} %bitcast.29, bf16[1,1024,2048]{2,1,0:T(8,128)(2,1)} %param.13), kind=kOutput, calls=%fused_computation.2 | convolution fusion | flops 2150629376 | bytes 11534337 | tf_op jit(solution)/shard_map/skd,df->skf/dot_general | solution.py:50
  75.3 1.2 collective-permute-start
  76.5 46.3 %collective-permute-done = bf16[512,2048]{1,0:T(8,128)(2,1)S(1)} collective-permute-done((bf16[512,2048]{1,0:T(8,128)(2,1)}, bf16[512,2048]{1,0:T(8,128)(2,1)S(1)}, u32[]{:S(2)}, u32[]{:S(2)}) %collective-permute-start) | collective-permute-done | bytes 2097184 | tf_op jit(solution)/shard_map/ppermute | solution.py:10
  122.9 4.5 %and_select_fusion = bf16[512,2048]{1,0:T(8,128)(2,1)} fusion(bf16[512,2048]{1,0:T(8,128)(2,1)S(1)} %collective-permute-done, f32[512,2048]{1,0:T(8,128)} %get-tuple-element.12, pred[]{:T(512)S(6)} %eq.58), kind=kLoop, calls=%fused_computation.3 | loop fusion | flops 3145728 | bytes 8388609 | tf_op jit(solution)/shard_map/jit(_where)/select_n | solution.py:57
  127.4 5.2 %conditional.1 = (f32[512,1024]{1,0:T(8,128)S(1)}) conditional(s32[]{:T(128)} %convert_element_type.40, () %tuple.14, (bf16[512,2048]{1,0:T(8,128)(2,1)}, bf16[1024,2048]{1,0:T(8,128)(2,1)}) %tuple.20), branch_computations={%region_5.6_spmd, %region_6.7_spmd} | conditional | flops 2147483648 | bytes 8388616 | solution.py:72
  127.4 5.2 %fusion.11 = f32[512,1024]{1,0:T(8,128)S(1)} fusion(bf16[512,2048]{1,0:T(8,128)(2,1)} %get-tuple-element.4, bf16[1024,2048]{1,0:T(8,128)(2,1)} %get-tuple-element.8), kind=kOutput, calls=%fused_computation.26 | convolution fusion | flops 2147483648 | bytes 8388608 | tf_op jit(solution)/shard_map/cond/branch_1_fun/dot_general | solution.py:65
  132.6 54.6 %all_to_all.10 = f32[16,32,1024]{2,1,0:T(8,128)S(1)} all-to-all(f32[16,32,1024]{2,1,0:T(8,128)S(1)} %bitcast.26), channel_id=1, replica_groups=mesh['section'=2,'dp'=16] {'dp'}, dimensions={0} | all-to-all | bytes 4194304 | tf_op jit(solution)/shard_map/all_to_all | solution.py:74
  187.2 0.0 copy-start
  187.2 0.2 bitcast_reduce_fusion
  187.4 0.5 convolution_convert_fusion.1
  187.9 1.3 collective-permute-start.1
  189.2 0.0 copy-done
  189.3 5.8 %convolution_bitcast_fusion = f32[1,1024,2048]{2,1,0:T(8,128)} fusion(bf16[512,1024]{1,0:T(8,128)(2,1)S(1)} %bitcast.30, bf16[512,2048]{1,0:T(8,128)(2,1)S(1)} %copy-done), kind=kOutput, calls=%fused_computation.1 | convolution fusion | flops 2147483648 | bytes 11534336 | tf_op jit(solution)/shard_map/dot_general | solution.py:60
  195.1 0.0 collective-permute-done.1
  195.1 0.7 slice_select_fusion
  (2 shorter events, 0.0 us)
Async XLA Ops:
  37.0 31.0 %all-to-all-start = ((bf16[16,32,1024]{2,1,0:T(8,128)(2,1)}), bf16[16,32,1024]{2,1,0:T(8,128)(2,1)S(1)}, u32[]{:S(2)}, u32[]{:S(2)}) async-start(bf16[16,32,1024]{2,1,0:T(8,128)(2,1)} %bitcast.3), calls=%async_computation | async-start | bytes 2097152 | tf_op jit(solution)/shard_map/all_to_all | solution.py:49
  75.3 47.6 %collective-permute-start = (bf16[512,2048]{1,0:T(8,128)(2,1)}, bf16[512,2048]{1,0:T(8,128)(2,1)S(1)}, u32[]{:S(2)}, u32[]{:S(2)}) collective-permute-start(bf16[512,2048]{1,0:T(8,128)(2,1)} %get-tuple-element.11), channel_id=1, source_target_pairs={{0,16},{16,0},{1,17},{17,1},{2,18},{18,2},{3,19},{19,3},{4,20},{20... | collective-permute-start | bytes 6291464 | tf_op jit(solution)/shard_map/ppermute | solution.py:10
  187.2 2.1 %copy-start = (bf16[512,2048]{1,0:T(8,128)(2,1)S(1)}, bf16[512,2048]{1,0:T(8,128)(2,1)}, u32[]{:S(2)}) copy-start(bf16[512,2048]{1,0:T(8,128)(2,1)} %and_select_fusion) | copy-start | bytes 6291460
  187.9 7.1 %collective-permute-start.1 = (bf16[128,512]{1,0:T(8,128)(2,1)S(1)}, bf16[128,512]{1,0:T(8,128)(2,1)S(1)}, u32[]{:S(2)}, u32[]{:S(2)}) collective-permute-start(bf16[128,512]{1,0:T(8,128)(2,1)S(1)} %slice.9), channel_id=1, source_target_pairs={{0,16},{1,17},{2,18},{3,19},{4,20},{5,21},{6,22},{7,23},{8,24},{9,... | collective-permute-start | bytes 393224 | tf_op jit(solution)/shard_map/ppermute | solution.py:16
where the time goes:
time: 196 us
  blocking collectives  85.2 us (43%)
  waiting for transfers between devices  69.5 us (35%)
  matrix products  20.1 us (10%)
  starting transfers between devices  10.4 us (5%)
  other arithmetic  8.72 us (4%)
    all_to_all x1, blocking collectives, on_device(): lax.all_to_all(partial_rows.reshape(replicas, capacity, row_width), 'dp',...  54.6 us
    ppermute x1, waiting for transfers between devices, partner(): return lax.ppermute(value, axis, pairs)  46.3 us
    psum x1, blocking collectives, on_device(): totals = lax.psum(lang_counts[0].astype(jnp.float32), 'dp')  30.6 us
    all_to_all x1, waiting for transfers between devices, on_device(): lax.all_to_all(doubled, 'dp', split_axis=0, concat_axis=0, tiled=True)  23.2 us
    all_to_all x1, starting transfers between devices, on_device(): lax.all_to_all(doubled, 'dp', split_axis=0, concat_axis=0, tiled=True)  7.84 us
    dot_general x1, matrix products, on_device(): jnp.einsum('skd,df->skf', arrived, own_weight, preferred_element_type=jnp...  7.29 us
    dot_general x1, matrix products, on_device(): lax.dot_general(routed_flat, partner_term, (((0,), (0,)), ((), ())), pref...  5.82 us
    dot_general x1, matrix products, input_terms(): lax.dot_general(partner_term, own_weight, (((1,), (1,)), ((), ())), prefe...  5.19 us
  transfers between devices with their start and end apart: 3, of which 2 were waited for; matrix products, arithmetic and copies ran while one was open for 3% of the time, Pallas kernels for 0%

commit v1 on v0

--- a/solution.py
+++ b/solution.py
@@ -35,7 +35,9 @@
     slot_index = jnp.sum(running * block_hot, axis=1)
     target = row_block * capacity + slot_index
     placing = target[None, :] == jnp.arange(blocks_all * capacity, dtype=jnp.int32)[:, None]
-    totals = lax.psum(lang_counts[0].astype(jnp.float32), "dp")
+    part = lang_counts[0].astype(jnp.float32)
+    parts = lax.all_gather(part, "dp")
+    totals = jnp.sum(parts, axis=0)
     lang_scale = 2.0 * replicas * temp_num.astype(jnp.float32) / totals
     row_scale = jnp.sum(jnp.where(lang_hot, lang_scale[None, :], 0.0), axis=1)
     local_rows = section_rows[0]

time: 196 us -> 184 us (0.939)
  blocking collectives: 85.2 us -> 77.6 us
  starting transfers between devices: 10.4 us -> 6.14 us
    psum x1 -> x0, blocking collectives: 30.6 us -> none  [on_device(): totals = lax.psum(lang_counts[0].astype(jnp.float32), 'dp')]
    all_gather x0 -> x1, blocking collectives: none -> 23 us  [on_device(): parts = lax.all_gather(part, 'dp')]
    all_to_all x1, starting transfers between devices: 7.84 us -> 3.63 us  [on_device(): lax.all_to_all(doubled, 'dp', split_axis=0, concat_axis=0, tiled=True)]
where the time goes in v1:
time: 184 us
  blocking collectives  77.6 us (42%)
  waiting for transfers between devices  69.5 us (38%)
  matrix products  20.1 us (11%)
  other arithmetic  8.76 us (5%)
  starting transfers between devices  6.14 us (3%)
    all_to_all x1, blocking collectives, on_device(): lax.all_to_all(partial_rows.reshape(replicas, capacity, row_width), 'dp',...  54.6 us
    ppermute x1, waiting for transfers between devices, partner(): return lax.ppermute(value, axis, pairs)  46.3 us
    all_to_all x1, waiting for transfers between devices, on_device(): lax.all_to_all(doubled, 'dp', split_axis=0, concat_axis=0, tiled=True)  23.2 us
    all_gather x1, blocking collectives, on_device(): parts = lax.all_gather(part, 'dp')  23 us
    dot_general x1, matrix products, on_device(): jnp.einsum('skd,df->skf', arrived, own_weight, preferred_element_type=jnp...  7.29 us
    dot_general x1, matrix products, on_device(): lax.dot_general(routed_flat, partner_term, (((0,), (0,)), ((), ())), pref...  5.82 us
    dot_general x1, matrix products, input_terms(): lax.dot_general(partner_term, own_weight, (((1,), (1,)), ((), ())), prefe...  5.19 us
    select_n x1, other arithmetic, on_device(): jnp.where((section_pos == 0) & (projected <= 0.0), jnp.zeros_like(receive...  4.5 us
  transfers between devices with their start and end apart: 3, of which 2 were waited for; matrix products, arithmetic and copies ran while one was open for 3% of the time, Pallas kernels for 0%

profile of v1, /device:TPU:1, one launch (start us, length us, event | category | flops | bytes accessed | tf_op | source)
XLA Modules:
  0.0 184.0 jit_solution(11045727502593928971)
XLA Ops:
  0.6 0.7 convert_bitcast_fusion
  1.3 23.0 %all-gather = f32[16,1,200]{2,1,0:T(1,128)S(1)} all-gather(f32[1,1,200]{2,1,0:T(1,128)S(1)} %convert_bitcast_fusion), channel_id=1, replica_groups=mesh['section'=2,'dp'=16] {'dp'}, dimensions={0}, use_global_device_ids=true | all-gather | bytes 13600 | tf_op jit(solution)/shard_map/all_gather | solution.py:39
  24.3 0.8 select_reduce_fusion.1
  25.1 0.7 multiply_divide_fusion
  25.8 0.8 select_reduce_fusion
  26.5 0.1 fusion.8
  26.6 0.2 reduce_window_sum.11
  26.8 0.2 select_reduce_fusion.2
  27.0 1.3 convolution_convert_fusion
  28.3 1.1 broadcast_in_dim.46
  29.4 3.6 %all-to-all-start = ((bf16[16,32,1024]{2,1,0:T(8,128)(2,1)}), bf16[16,32,1024]{2,1,0:T(8,128)(2,1)S(1)}, u32[]{:S(2)}, u32[]{:S(2)}) async-start(bf16[16,32,1024]{2,1,0:T(8,128)(2,1)} %bitcast.3), calls=%async_computation | async-start | bytes 2097152 | tf_op jit(solution)/shard_map/all_to_all | solution.py:51
  33.1 23.2 %all-to-all-done = bf16[16,32,1024]{2,1,0:T(8,128)(2,1)S(1)} async-done(((bf16[16,32,1024]{2,1,0:T(8,128)(2,1)}), bf16[16,32,1024]{2,1,0:T(8,128)(2,1)S(1)}, u32[]{:S(2)}, u32[]{:S(2)}) %all-to-all-start) | async-done | bytes 1048608 | tf_op jit(solution)/shard_map/all_to_all | solution.py:51
  56.3 7.3 %fusion = (bf16[512,2048]{1,0:T(8,128)(2,1)}, f32[512,2048]{1,0:T(8,128)}) fusion(pred[]{:T(512)S(6)} %eq.58, bf16[512,1024]{1,0:T(8,128)(2,1)S(1)} %bitcast.30, bf16[1,1024,2048]{2,1,0:T(8,128)(2,1)} %param.13), kind=kOutput, calls=%fused_computation.2 | convolution fusion | flops 2150629376 | bytes 11534337 | tf_op jit(solution)/shard_map/skd,df->skf/dot_general | solution.py:52
  63.5 1.2 collective-permute-start
  64.8 46.3 %collective-permute-done = bf16[512,2048]{1,0:T(8,128)(2,1)S(1)} collective-permute-done((bf16[512,2048]{1,0:T(8,128)(2,1)}, bf16[512,2048]{1,0:T(8,128)(2,1)S(1)}, u32[]{:S(2)}, u32[]{:S(2)}) %collective-permute-start) | collective-permute-done | bytes 2097184 | tf_op jit(solution)/shard_map/ppermute | solution.py:10
  111.1 4.5 %and_select_fusion = bf16[512,2048]{1,0:T(8,128)(2,1)} fusion(bf16[512,2048]{1,0:T(8,128)(2,1)S(1)} %collective-permute-done, f32[512,2048]{1,0:T(8,128)} %get-tuple-element.12, pred[]{:T(512)S(6)} %eq.58), kind=kLoop, calls=%fused_computation.3 | loop fusion | flops 3145728 | bytes 8388609 | tf_op jit(solution)/shard_map/jit(_where)/select_n | solution.py:59
  115.6 5.2 %conditional.1 = (f32[512,1024]{1,0:T(8,128)S(1)}) conditional(s32[]{:T(128)} %convert_element_type.37, () %tuple.14, (bf16[512,2048]{1,0:T(8,128)(2,1)}, bf16[1024,2048]{1,0:T(8,128)(2,1)}) %tuple.20), branch_computations={%region_5.6_spmd, %region_6.7_spmd} | conditional | flops 2147483648 | bytes 8388616 | solution.py:74
  115.6 5.2 %fusion.11 = f32[512,1024]{1,0:T(8,128)S(1)} fusion(bf16[512,2048]{1,0:T(8,128)(2,1)} %get-tuple-element.4, bf16[1024,2048]{1,0:T(8,128)(2,1)} %get-tuple-element.8), kind=kOutput, calls=%fused_computation.27 | convolution fusion | flops 2147483648 | bytes 8388608 | tf_op jit(solution)/shard_map/cond/branch_1_fun/dot_general | solution.py:67
  120.8 54.6 %all_to_all.10 = f32[16,32,1024]{2,1,0:T(8,128)S(1)} all-to-all(f32[16,32,1024]{2,1,0:T(8,128)S(1)} %bitcast.27), channel_id=1, replica_groups=mesh['section'=2,'dp'=16] {'dp'}, dimensions={0} | all-to-all | bytes 4194304 | tf_op jit(solution)/shard_map/all_to_all | solution.py:76
  175.4 0.0 copy-start
  175.4 0.2 bitcast_reduce_fusion
  175.6 0.5 convolution_convert_fusion.1
  176.2 1.3 collective-permute-start.1
  177.5 0.0 copy-done
  177.5 5.8 %convolution_bitcast_fusion = f32[1,1024,2048]{2,1,0:T(8,128)} fusion(bf16[512,1024]{1,0:T(8,128)(2,1)S(1)} %bitcast.31, bf16[512,2048]{1,0:T(8,128)(2,1)S(1)} %copy-done), kind=kOutput, calls=%fused_computation.1 | convolution fusion | flops 2147483648 | bytes 11534336 | tf_op jit(solution)/shard_map/dot_general | solution.py:62
  183.3 0.0 collective-permute-done.1
  183.3 0.7 slice_select_fusion
  (3 shorter events, 0.1 us)
Async XLA Ops:
  29.4 26.8 %all-to-all-start = ((bf16[16,32,1024]{2,1,0:T(8,128)(2,1)}), bf16[16,32,1024]{2,1,0:T(8,128)(2,1)S(1)}, u32[]{:S(2)}, u32[]{:S(2)}) async-start(bf16[16,32,1024]{2,1,0:T(8,128)(2,1)} %bitcast.3), calls=%async_computation | async-start | bytes 2097152 | tf_op jit(solution)/shard_map/all_to_all | solution.py:51
  63.5 47.6 %collective-permute-start = (bf16[512,2048]{1,0:T(8,128)(2,1)}, bf16[512,2048]{1,0:T(8,128)(2,1)S(1)}, u32[]{:S(2)}, u32[]{:S(2)}) collective-permute-start(bf16[512,2048]{1,0:T(8,128)(2,1)} %get-tuple-element.11), channel_id=1, source_target_pairs={{0,16},{16,0},{1,17},{17,1},{2,18},{18,2},{3,19},{19,3},{4,20},{20... | collective-permute-start | bytes 6291464 | tf_op jit(solution)/shard_map/ppermute | solution.py:10
  175.4 2.1 %copy-start = (bf16[512,2048]{1,0:T(8,128)(2,1)S(1)}, bf16[512,2048]{1,0:T(8,128)(2,1)}, u32[]{:S(2)}) copy-start(bf16[512,2048]{1,0:T(8,128)(2,1)} %and_select_fusion) | copy-start | bytes 6291460
  176.2 7.1 %collective-permute-start.1 = (bf16[128,512]{1,0:T(8,128)(2,1)S(1)}, bf16[128,512]{1,0:T(8,128)(2,1)S(1)}, u32[]{:S(2)}, u32[]{:S(2)}) collective-permute-start(bf16[128,512]{1,0:T(8,128)(2,1)S(1)} %slice.9), channel_id=1, source_target_pairs={{0,16},{1,17},{2,18},{3,19},{4,20},{5,21},{6,22},{7,23},{8,24},{9,... | collective-permute-start | bytes 393224 | tf_op jit(solution)/shard_map/ppermute | solution.py:16
